TPU v7x, 32 devices: a whole 2x2x4 slice. The times are simulated.
32 devices in a mesh: node: 16 (over z, y, core), chip: 2 (over x).
Axes of the slice: x: 2, y: 2, z: 4, core: 2. Of those that a mesh axis runs over, the one named last changes fastest.
Arguments:
- tokens: bfloat16 [256, 3584], P(('node', 'chip')), may hold values from -6 to 6
- expert_ids: int32 [256, 8], P(('node', 'chip')), may hold values from 0 to 31, as said below
- gate_values: bfloat16 [256, 8], P(('node', 'chip')), may hold values from 0.099609375 to 1
- slot_ids: int32 [256, 8], P(('node', 'chip')), may hold values from 0 to 7, as said below
- up_weight: bfloat16 [32, 3584, 1024], P('node', None, 'chip'), may hold values from -0.09375 to 0.09375
- down_weight: bfloat16 [32, 1024, 3584], P('node', 'chip'), may hold values from -0.1875 to 0.1875
Outputs:
- mixed: bfloat16 [256, 3584], P(('node', 'chip'))
Inputs may be any that keep to these rules, and one draw needn't show every extreme that they name: `expert_ids`: each token's 8 entries name, in some order, all 2 experts of each of 4 distinct nodes. `slot_ids`: entries of one token that name experts of the same node hold the same slot; among the 16 tokens of one node (aligned blocks of the token dimension), the slots to one destination node are distinct, and some destination node receives all 8 slots from each source node.
All inputs are finite; a program needn't handle non-finite values.
Results may differ from a plain program's by a relative error of at most 0.0058.
Values may be sent and summed in bfloat16 or wider, within the bound.
A program may use at most 64 MiB of HBM per device.

v0:
```python
import jax
import jax.numpy as jnp
from jax import lax
from jax.sharding import PartitionSpec as P


def pack_rows(targets, experts, node_tokens, node_gates, row_count, per_node):
    row_ids = jnp.arange(row_count, dtype=jnp.int32)
    matches = (targets[None, :, :] == row_ids[:, None, None]).astype(jnp.bfloat16)
    picked = jnp.minimum(jnp.sum(matches.astype(jnp.float32), axis=2), 1.0).astype(jnp.bfloat16)
    packed = jnp.dot(picked, node_tokens, preferred_element_type=jnp.float32).astype(jnp.bfloat16)
    choose = (experts[:, :, None] == jnp.arange(per_node, dtype=jnp.int32)[None, None, :]).astype(
        jnp.bfloat16
    )
    weighted = choose * node_gates[:, :, None]
    gate_rows = jnp.einsum(
        "rtk,tke->re", matches, weighted, preferred_element_type=jnp.float32
    ).astype(jnp.bfloat16)
    return (packed, gate_rows)


def expert_rows(row_block, gate_block, up_local, down_local):
    result = jnp.zeros((row_block.shape[0], down_local.shape[2]), jnp.float32)
    for expert in range(up_local.shape[0]):
        hidden = jax.nn.silu(
            jnp.dot(row_block, up_local[expert], preferred_element_type=jnp.float32)
        ).astype(jnp.bfloat16)
        product = jnp.dot(hidden, down_local[expert], preferred_element_type=jnp.float32)
        result = result + gate_block[:, expert : expert + 1].astype(jnp.float32) * product
    return result.astype(jnp.bfloat16)


def gather_sum(indices, table):
    valid = indices >= 0
    safe = jnp.where(valid, indices, 0).reshape(-1)
    picked = jnp.take(table, safe, axis=0).reshape(
        indices.shape[0], indices.shape[1], table.shape[1]
    )
    return jnp.sum(jnp.where(valid[:, :, None], picked, 0.0), axis=1)


def shards(tokens, expert_ids, gate_values, slot_ids, up_weight, down_weight):
    node_count = lax.axis_size("node")
    chip_count = lax.axis_size("chip")
    my_chip = lax.axis_index("chip")
    tok_dev = tokens.shape[0]
    model_dim = tokens.shape[1]
    per_node = up_weight.shape[0]
    capacity = 8 * chip_count * tok_dev // node_count
    block_cap = capacity // chip_count
    route_code = (expert_ids // per_node * capacity + slot_ids) * per_node + expert_ids % per_node
    node_tokens, node_gates = (
        lax.all_gather(tokens, "chip", axis=0, tiled=True),
        lax.all_gather(gate_values, "chip", axis=0, tiled=True),
    )
    node_codes = lax.all_gather(route_code, "chip", axis=0, tiled=True)
    node_expert = node_codes % per_node
    node_slot = node_codes // per_node % capacity
    node_dest = node_codes // per_node // capacity
    targets = node_dest * capacity + node_slot
    packed, gate_rows = pack_rows(
        targets, node_expert, node_tokens, node_gates, node_count * capacity, per_node
    )
    shaped = packed.reshape(node_count, chip_count, 1, block_cap, model_dim)
    gate_shaped = gate_rows.reshape(node_count, chip_count, 1, block_cap, per_node)
    arrived, arrived_gates = (
        lax.all_to_all(shaped, "node", split_axis=0, concat_axis=2, tiled=True),
        lax.all_to_all(gate_shaped, "node", split_axis=0, concat_axis=2, tiled=True),
    )
    row_block = arrived.reshape(-1, model_dim)
    gate_block = arrived_gates.reshape(-1, per_node)
    partial_value = expert_rows(row_block, gate_block, up_weight, down_weight)
    pieces = lax.all_to_all(
        partial_value.reshape(chip_count, node_count * block_cap, model_dim),
        "chip",
        split_axis=0,
        concat_axis=0,
        tiled=True,
    )
    slot_sums = jnp.sum(pieces.astype(jnp.float32), axis=0).reshape(
        node_count, block_cap, model_dim
    )
    held = lax.all_to_all(slot_sums, "node", split_axis=0, concat_axis=0, tiled=True).reshape(
        node_count * block_cap, model_dim
    )
    wanted = (node_slot // block_cap == my_chip) & (node_expert == 0)
    indices = jnp.where(wanted, node_dest * block_cap + node_slot % block_cap, -1)
    term = gather_sum(indices, held)
    summed = lax.psum_scatter(term, "chip", scatter_dimension=0, tiled=True)
    return summed.astype(jnp.bfloat16)


def solution(mesh):
    return jax.shard_map(
        shards,
        mesh=mesh,
        in_specs=(
            P(("node", "chip"), None),
            P(("node", "chip"), None),
            P(("node", "chip"), None),
            P(("node", "chip"), None),
            P("node", None, "chip"),
            P("node", "chip", None),
        ),
        out_specs=P(("node", "chip"), None),
        check_vma=False,
    )
```

profile of v0, /device:TPU:0, one launch (start us, length us, event | category | flops | bytes accessed | tf_op | source)
XLA Modules:
  0.0 136.6 jit_solution(9596992641009980675)
XLA Ops:
  6.5 0.7 fusion.38
  7.3 5.3 %all_gather.9 = s32[16,8]{1,0:T(8,128)S(1)} all-gather(s32[8,8]{1,0:T(8,128)S(1)} %fusion.38), channel_id=1, replica_groups=mesh['node'=16,'chip'=2] {'chip'}, dimensions={0}, use_global_device_ids=true | all-gather | bytes 768 | tf_op jit(solution)/shard_map/all_gather | solution.py:56
  12.5 4.6 %all_gather.10 = bf16[16,8]{1,0:T(8,128)(2,1)S(1)} all-gather(bf16[8,8]{1,0:T(8,128)(2,1)} %param.8), channel_id=1, replica_groups=mesh['node'=16,'chip'=2] {'chip'}, dimensions={0}, use_global_device_ids=true | all-gather | bytes 384 | tf_op jit(solution)/shard_map/all_gather | solution.py:54
  17.1 0.1 copy.18
  17.2 0.1 copy.17
  17.3 0.1 copy.16
  17.4 0.2 fusion.14
  17.6 0.1 reshape.70
  17.7 0.6 copy.19
  18.3 6.4 %all-to-all-start = ((bf16[16,2,1,4,2]{3,1,4,2,0:T(2,128)(2,1)}), bf16[16,2,1,4,2]{3,1,4,2,0:T(2,128)(2,1)S(1)}, u32[]{:S(2)}, u32[]{:S(2)}) async-start(bf16[16,2,1,4,2]{3,1,4,2,0:T(2,128)(2,1)} %copy.19), calls=%async_computation | async-start | bytes 32768 | tf_op jit(solution)/shard_map/all_to_all | solution.py:68
  24.7 0.1 convert_reduce_fusion.1
  24.8 5.1 %all_gather.11 = bf16[16,3584]{1,0:T(8,128)(2,1)S(1)} all-gather(bf16[8,3584]{1,0:T(8,128)(2,1)} %param.6), channel_id=1, replica_groups=mesh['node'=16,'chip'=2] {'chip'}, dimensions={0}, use_global_device_ids=true | all-gather | bytes 172032 | tf_op jit(solution)/shard_map/all_gather | solution.py:53
  29.9 0.4 convolution_convert_fusion
  30.4 1.1 reshape.72
  31.5 0.0 all-to-all-done
  31.5 6.0 %all-to-all-start.1 = ((bf16[16,2,1,4,3584]{4,3,1,2,0:T(4,128)(2,1)}), bf16[16,2,1,4,3584]{4,3,1,2,0:T(4,128)(2,1)S(1)}, u32[]{:S(2)}, u32[]{:S(2)}) async-start(bf16[16,2,1,4,3584]{4,3,1,2,0:T(4,128)(2,1)} %bitcast.4), calls=%async_computation.1 | async-start | bytes 1835008 | tf_op jit(solution)/shard_map/all_to_all | solution.py:67
  37.5 0.1 reshape.71
  37.6 20.6 %all-to-all-done.1 = bf16[16,2,1,4,3584]{4,3,1,2,0:T(4,128)(2,1)S(1)} async-done(((bf16[16,2,1,4,3584]{4,3,1,2,0:T(4,128)(2,1)}), bf16[16,2,1,4,3584]{4,3,1,2,0:T(4,128)(2,1)S(1)}, u32[]{:S(2)}, u32[]{:S(2)}) %all-to-all-start.1) | async-done | bytes 917536 | tf_op jit(solution)/shard_map/all_to_all | solution.py:67
  58.3 0.3 copy.22
  58.6 0.2 reshape.73
  58.8 5.7 %convolution_multiply_fusion.1 = f32[128,3584]{1,0:T(8,128)} fusion(bf16[2,512,3584]{2,1,0:T(8,128)(2,1)} %param.11, f32[128]{0:T(128)S(1)} %get-tuple-element.10, bf16[128,3584]{1,0:T(8,128)(2,1)S(1)} %reshape.73, bf16[2,3584,512]{2,1,0:T(8,128)(2,1)} %param.10), kind=kOutput, calls=%fused_computation.3 | convolution fusion | flops 940310528 | bytes 10093056 | tf_op jit(solution)/shard_map/dot_general | solution.py:28
  64.5 4.9 %fusion.1 = bf16[128,3584]{1,0:T(8,128)(2,1)S(1)} fusion(f32[128,3584]{1,0:T(8,128)} %convolution_multiply_fusion.1, bf16[2,512,3584]{2,1,0:T(8,128)(2,1)} %param.11, f32[128]{0:T(128)S(1)} %get-tuple-element.9, bf16[128,3584]{1,0:T(8,128)(2,1)S(1)} %reshape.73, bf16[2,3584,512]{2,1,0:T(8,128)(2,1)} %param.10), kind=kOutput, calls=%fused_computation.4 | convolution fusion | flops 941228032 | bytes 11010560 | tf_op jit(solution)/shard_map/dot_general | solution.py:28
  69.5 15.6 %all_to_all.40 = bf16[2,64,3584]{2,1,0:T(8,128)(2,1)S(1)} all-to-all(bf16[2,64,3584]{2,1,0:T(8,128)(2,1)S(1)} %bitcast.58), channel_id=1, replica_groups=mesh['node'=16,'chip'=2] {'chip'}, dimensions={0} | all-to-all | bytes 1835008 | tf_op jit(solution)/shard_map/all_to_all | solution.py:73
  85.1 0.1 convert_reduce_fusion
  85.2 1.2 reshape.75
  86.4 5.9 %all-to-all-start.3 = ((f32[16,4,3584]{2,1,0:T(4,128)}), f32[16,4,3584]{2,1,0:T(4,128)S(1)}, u32[]{:S(2)}, u32[]{:S(2)}) async-start(f32[16,4,3584]{2,1,0:T(4,128)} %reshape.75), calls=%async_computation.3 | async-start | bytes 1835008 | tf_op jit(solution)/shard_map/all_to_all | solution.py:83
  92.4 0.0 reduce-scatter.2.cloned.1.call-start
  92.5 0.1 reshape.77
  92.6 20.5 %all-to-all-done.3 = f32[16,4,3584]{2,1,0:T(4,128)S(1)} async-done(((f32[16,4,3584]{2,1,0:T(4,128)}), f32[16,4,3584]{2,1,0:T(4,128)S(1)}, u32[]{:S(2)}, u32[]{:S(2)}) %all-to-all-start.3) | async-done | bytes 917536 | tf_op jit(solution)/shard_map/all_to_all | solution.py:83
  113.1 0.3 reshape.76
  113.5 1.3 gather_fusion
  114.7 1.4 %fusion.13 = f32[16,3584]{1,0:T(8,128)} fusion(f32[128,3584]{1,0:T(8,128)S(1)} %gather_fusion, pred[16,8]{1,0:T(8,128)(4,1)S(1)} %compare_and_fusion, pred[16,8]{1,0:T(8,128)(4,1)S(1)} %get-tuple-element.5), kind=kLoop, calls=%fused_computation.18 | loop fusion | flops 1318912 | bytes 2064640 | tf_op jit(solution)/shard_map/reduce_sum | solution.py:39
  116.2 0.0 reduce-scatter.2.cloned.1.call-update
  116.2 12.0 %reduce-scatter.2.cloned.1.call-done = f32[8,3584]{1,0:T(8,128)} async-done(((f32[16,3584]{1,0:T(8,128)}), f32[8,3584]{1,0:T(8,128)}) %reduce-scatter.2.cloned.1.call-update) | async-done | bytes 114704 | tf_op jit(solution)/shard_map/reduce_scatter | solution.py:89
  128.2 1.5 %convert_element_type.42 = bf16[8,3584]{1,0:T(8,128)(2,1)} convert(f32[8,3584]{1,0:T(8,128)} %reduce-scatter.2.cloned.1.call-done) | non-fusion elementwise | flops 28672 | bytes 172032 | tf_op jit(solution)/shard_map/convert_element_type | solution.py:90
  (8 shorter events, 0.1 us)
Async XLA Ops:
  18.3 13.2 %all-to-all-start = ((bf16[16,2,1,4,2]{3,1,4,2,0:T(2,128)(2,1)}), bf16[16,2,1,4,2]{3,1,4,2,0:T(2,128)(2,1)S(1)}, u32[]{:S(2)}, u32[]{:S(2)}) async-start(bf16[16,2,1,4,2]{3,1,4,2,0:T(2,128)(2,1)} %copy.19), calls=%async_computation | async-start | bytes 32768 | tf_op jit(solution)/shard_map/all_to_all | solution.py:68
  31.5 26.8 %all-to-all-start.1 = ((bf16[16,2,1,4,3584]{4,3,1,2,0:T(4,128)(2,1)}), bf16[16,2,1,4,3584]{4,3,1,2,0:T(4,128)(2,1)S(1)}, u32[]{:S(2)}, u32[]{:S(2)}) async-start(bf16[16,2,1,4,3584]{4,3,1,2,0:T(4,128)(2,1)} %bitcast.4), calls=%async_computation.1 | async-start | bytes 1835008 | tf_op jit(solution)/shard_map/all_to_all | solution.py:67
  86.4 26.7 %all-to-all-start.3 = ((f32[16,4,3584]{2,1,0:T(4,128)}), f32[16,4,3584]{2,1,0:T(4,128)S(1)}, u32[]{:S(2)}, u32[]{:S(2)}) async-start(f32[16,4,3584]{2,1,0:T(4,128)} %reshape.75), calls=%async_computation.3 | async-start | bytes 1835008 | tf_op jit(solution)/shard_map/all_to_all | solution.py:83
  92.4 35.9 %reduce-scatter.2.cloned.1.call-start = ((), (), s32[]{:S(2)}) async-start(), calls=%async_computation.5 | async-start | bytes 344064 | tf_op jit(solution)/shard_map/reduce_scatter | solution.py:89
Sparse Core Ops, SparseCore 0:
  116.3 11.8 reduce-scatter.1
where the time goes:
time: 137 us
  waiting for transfers between devices  53.3 us (39%)
  blocking collectives  30.6 us (22%)
  starting transfers between devices  18.4 us (13%)
  between operations  13.5 us (10%)
  matrix products  11.3 us (8%)
  local copies, waits for them, and re-layouts  5.6 us (4%)
  other arithmetic  3.99 us (3%)
    all_to_all x1, waiting for transfers between devices, shards(): lax.all_to_all(shaped, 'node', split_axis=0, concat_axis=2, tiled=True)  20.6 us
    all_to_all x1, waiting for transfers between devices, shards(): lax.all_to_all(slot_sums, 'node', split_axis=0, concat_axis=0, tiled=True)  20.5 us
    all_to_all x1, blocking collectives, shards(): lax.all_to_all(partial_value.reshape(chip_count, node_count * block_cap,...  15.6 us
    reduce_scatter x1, waiting for transfers between devices, shards(): summed = lax.psum_scatter(term, 'chip', scatter_dimension=0, tiled=True)  12 us
    dot_general x2, matrix products, expert_rows(): jnp.dot(hidden, down_local[expert], preferred_element_type=jnp.float32)  10.7 us
    all_to_all x1, starting transfers between devices, shards(): lax.all_to_all(gate_shaped, 'node', split_axis=0, concat_axis=2, tiled=True)  6.42 us
    all_to_all x1, starting transfers between devices, shards(): lax.all_to_all(shaped, 'node', split_axis=0, concat_axis=2, tiled=True)  5.97 us
    all_to_all x1, starting transfers between devices, shards(): lax.all_to_all(slot_sums, 'node', split_axis=0, concat_axis=0, tiled=True)  5.95 us
  transfers between devices with their start and end apart: 4, of which 3 were waited for; matrix products, arithmetic and copies ran while one was open for 1% of the time, Pallas kernels for 0%

commit v1 on v0

--- a/solution.py
+++ b/solution.py
@@ -63,8 +63,17 @@
     )
     shaped = packed.reshape(node_count, chip_count, 1, block_cap, model_dim)
     gate_shaped = gate_rows.reshape(node_count, chip_count, 1, block_cap, per_node)
+    _bind_indices = lambda vals, k_dim, axis_k: jnp.concatenate(
+        lax.all_to_all(
+            jnp.stack(jnp.split(vals, lax.axis_size("node"), axis=k_dim)),
+            axis_name="node",
+            split_axis=0,
+            concat_axis=0,
+        ),
+        axis=axis_k,
+    )
     arrived, arrived_gates = (
-        lax.all_to_all(shaped, "node", split_axis=0, concat_axis=2, tiled=True),
+        _bind_indices(shaped, 0, 2),
         lax.all_to_all(gate_shaped, "node", split_axis=0, concat_axis=2, tiled=True),
     )
     row_block = arrived.reshape(-1, model_dim)

time: 137 us -> 147 us (1.073)
  local copies, waits for them, and re-layouts: 5.6 us -> 15.1 us
    unnamed x0 -> x15, local copies, waits for them, and re-layouts: none -> 9.59 us
  transfers between devices with their start and end apart: 4 -> 4, of which waited for: 3 -> 3; matrix products, arithmetic and copies ran while one was open for 1% -> 8% of each run, Pallas kernels for 0% -> 0%
where the time goes in v1:
time: 147 us; the launch traced here: 146 us
  waiting for transfers between devices  53.3 us (36%)
  blocking collectives  30.6 us (21%)
  starting transfers between devices  18.4 us (13%)
  local copies, waits for them, and re-layouts  15.1 us (10%)
  between operations  13.6 us (9%)
  matrix products  11.3 us (8%)
  other arithmetic  4 us (3%)
    all_to_all x1, waiting for transfers between devices, shards(): lax.all_to_all(jnp.stack(jnp.split(vals, lax.axis_size('node'), axis=k_di...  20.6 us
    all_to_all x1, waiting for transfers between devices, shards(): lax.all_to_all(slot_sums, 'node', split_axis=0, concat_axis=0, tiled=True)  20.5 us
    all_to_all x1, blocking collectives, shards(): lax.all_to_all(partial_value.reshape(chip_count, node_count * block_cap,...  15.6 us
    reduce_scatter x1, waiting for transfers between devices, shards(): summed = lax.psum_scatter(term, 'chip', scatter_dimension=0, tiled=True)  12 us
    dot_general x2, matrix products, expert_rows(): jnp.dot(hidden, down_local[expert], preferred_element_type=jnp.float32)  10.7 us
    unnamed x15, local copies, waits for them, and re-layouts  9.59 us
    all_to_all x1, starting transfers between devices, shards(): lax.all_to_all(gate_shaped, 'node', split_axis=0, concat_axis=2, tiled=True)  6.42 us
    all_to_all x1, starting transfers between devices, shards(): lax.all_to_all(jnp.stack(jnp.split(vals, lax.axis_size('node'), axis=k_di...  5.97 us
  transfers between devices with their start and end apart: 4, of which 3 were waited for; matrix products, arithmetic and copies ran while one was open for 8% of the time, Pallas kernels for 0%

profile of v1, /device:TPU:0, one launch (start us, length us, event | category | flops | bytes accessed | tf_op | source)
XLA Modules:
  0.0 146.2 jit_solution(2274132439537289467)
XLA Ops:
  6.5 0.7 fusion.38
  7.3 5.3 %all_gather.9 = s32[16,8]{1,0:T(8,128)S(1)} all-gather(s32[8,8]{1,0:T(8,128)S(1)} %fusion.38), channel_id=1, replica_groups=mesh['node'=16,'chip'=2] {'chip'}, dimensions={0}, use_global_device_ids=true | all-gather | bytes 768 | tf_op jit(solution)/shard_map/all_gather | solution.py:56
  12.5 4.6 %all_gather.10 = bf16[16,8]{1,0:T(8,128)(2,1)S(1)} all-gather(bf16[8,8]{1,0:T(8,128)(2,1)} %param.8), channel_id=1, replica_groups=mesh['node'=16,'chip'=2] {'chip'}, dimensions={0}, use_global_device_ids=true | all-gather | bytes 384 | tf_op jit(solution)/shard_map/all_gather | solution.py:54
  17.1 0.1 copy.33
  17.2 0.1 copy.32
  17.3 0.1 copy.31
  17.4 0.2 fusion.14
  17.6 0.1 reshape.99
  17.7 0.6 copy.34
  18.3 6.4 %all-to-all-start = ((bf16[16,2,1,4,2]{3,1,4,2,0:T(2,128)(2,1)}), bf16[16,2,1,4,2]{3,1,4,2,0:T(2,128)(2,1)S(1)}, u32[]{:S(2)}, u32[]{:S(2)}) async-start(bf16[16,2,1,4,2]{3,1,4,2,0:T(2,128)(2,1)} %copy.34), calls=%async_computation | async-start | bytes 32768 | tf_op jit(solution)/shard_map/all_to_all | solution.py:77
  24.7 0.1 convert_reduce_fusion.1
  24.8 5.1 %all_gather.11 = bf16[16,3584]{1,0:T(8,128)(2,1)S(1)} all-gather(bf16[8,3584]{1,0:T(8,128)(2,1)} %param.6), channel_id=1, replica_groups=mesh['node'=16,'chip'=2] {'chip'}, dimensions={0}, use_global_device_ids=true | all-gather | bytes 172032 | tf_op jit(solution)/shard_map/all_gather | solution.py:53
  29.9 0.4 convolution_convert_fusion
  30.4 0.1 fusion.53
  30.8 0.6 constant_dynamic-update-slice_fusion.15
  31.4 0.6 constant_dynamic-update-slice_fusion.14
  32.1 0.6 constant_dynamic-update-slice_fusion.13
  32.7 0.6 constant_dynamic-update-slice_fusion.12
  33.4 0.6 constant_dynamic-update-slice_fusion.11
  34.0 0.7 constant_dynamic-update-slice_fusion.10
  34.6 0.6 constant_dynamic-update-slice_fusion.9
  35.3 0.6 constant_dynamic-update-slice_fusion.8
  35.9 0.6 constant_dynamic-update-slice_fusion.7
  36.6 0.7 constant_dynamic-update-slice_fusion.6
  37.2 0.6 constant_dynamic-update-slice_fusion.5
  37.8 0.6 constant_dynamic-update-slice_fusion.4
  38.5 0.6 constant_dynamic-update-slice_fusion.3
  39.1 0.6 constant_dynamic-update-slice_fusion.2
  39.8 0.7 constant_dynamic-update-slice_fusion.1
  40.4 0.6 constant_dynamic-update-slice_fusion
  41.1 6.0 %all-to-all-start.1 = ((bf16[16,1,2,1,4,3584]{5,4,2,3,1,0:T(4,128)(2,1)}), bf16[16,1,2,1,4,3584]{5,4,2,3,1,0:T(4,128)(2,1)S(1)}, u32[]{:S(2)}, u32[]{:S(2)}) async-start(bf16[16,1,2,1,4,3584]{5,4,2,3,1,0:T(4,128)(2,1)} %constant_dynamic-update-slice_fusion), calls=%async_computation.1 | async-start | bytes 1835008 | tf_op jit(solution)/shard_map/all_to_all | solution.py:67
  47.0 0.1 reshape.100
  47.2 20.6 %all-to-all-done.1 = bf16[16,1,2,1,4,3584]{5,4,2,3,1,0:T(4,128)(2,1)S(1)} async-done(((bf16[16,1,2,1,4,3584]{5,4,2,3,1,0:T(4,128)(2,1)}), bf16[16,1,2,1,4,3584]{5,4,2,3,1,0:T(4,128)(2,1)S(1)}, u32[]{:S(2)}, u32[]{:S(2)}) %all-to-all-start.1) | async-done | bytes 917536 | tf_op jit(solution)/shard_map/all_to_all | solution.py:67
  67.8 0.3 copy.36
  68.1 0.2 reshape_reshape.3
  68.3 5.7 %convolution_multiply_fusion.1 = f32[128,3584]{1,0:T(8,128)} fusion(bf16[2,512,3584]{2,1,0:T(8,128)(2,1)} %param.11, f32[128]{0:T(128)S(1)} %get-tuple-element.26, bf16[128,3584]{1,0:T(8,128)(2,1)S(1)} %reshape_reshape.3, bf16[2,3584,512]{2,1,0:T(8,128)(2,1)} %param.10), kind=kOutput, calls=%fused_computation.3 | convolution fusion | flops 940310528 | bytes 10093056 | tf_op jit(solution)/shard_map/dot_general | solution.py:28
  74.1 5.0 %fusion.1 = bf16[128,3584]{1,0:T(8,128)(2,1)S(1)} fusion(f32[128,3584]{1,0:T(8,128)} %convolution_multiply_fusion.1, bf16[2,512,3584]{2,1,0:T(8,128)(2,1)} %param.11, f32[128]{0:T(128)S(1)} %get-tuple-element.25, bf16[128,3584]{1,0:T(8,128)(2,1)S(1)} %reshape_reshape.3, bf16[2,3584,512]{2,1,0:T(8,128)(2,1)} %param.10), kind=kOutput, calls=%fused_computation.4 | convolution fusion | flops 941228032 | bytes 11010560 | tf_op jit(solution)/shard_map/dot_general | solution.py:28
  79.0 15.6 %all_to_all.30 = bf16[2,64,3584]{2,1,0:T(8,128)(2,1)S(1)} all-to-all(bf16[2,64,3584]{2,1,0:T(8,128)(2,1)S(1)} %bitcast.55), channel_id=1, replica_groups=mesh['node'=16,'chip'=2] {'chip'}, dimensions={0} | all-to-all | bytes 1835008 | tf_op jit(solution)/shard_map/all_to_all | solution.py:82
  94.6 0.1 convert_reduce_fusion
  94.8 1.2 reshape.103
  96.0 5.9 %all-to-all-start.3 = ((f32[16,4,3584]{2,1,0:T(4,128)}), f32[16,4,3584]{2,1,0:T(4,128)S(1)}, u32[]{:S(2)}, u32[]{:S(2)}) async-start(f32[16,4,3584]{2,1,0:T(4,128)} %reshape.103), calls=%async_computation.3 | async-start | bytes 1835008 | tf_op jit(solution)/shard_map/all_to_all | solution.py:92
  102.0 0.1 reshape.105
  102.1 20.5 %all-to-all-done.3 = f32[16,4,3584]{2,1,0:T(4,128)S(1)} async-done(((f32[16,4,3584]{2,1,0:T(4,128)}), f32[16,4,3584]{2,1,0:T(4,128)S(1)}, u32[]{:S(2)}, u32[]{:S(2)}) %all-to-all-start.3) | async-done | bytes 917536 | tf_op jit(solution)/shard_map/all_to_all | solution.py:92
  122.7 0.3 reshape.104
  123.0 1.3 gather_fusion
  124.3 1.4 fusion.13
  125.8 12.0 %reduce-scatter.2.cloned.1.call-done = f32[8,3584]{1,0:T(8,128)} async-done(((f32[16,3584]{1,0:T(8,128)}), f32[8,3584]{1,0:T(8,128)}) %reduce-scatter.2.cloned.1.call-update) | async-done | bytes 114704 | tf_op jit(solution)/shard_map/reduce_scatter | solution.py:98
  137.8 1.5 %convert_element_type.42 = bf16[8,3584]{1,0:T(8,128)(2,1)} convert(f32[8,3584]{1,0:T(8,128)} %reduce-scatter.2.cloned.1.call-done) | non-fusion elementwise | flops 28672 | bytes 172032 | tf_op jit(solution)/shard_map/convert_element_type | solution.py:99
  (27 shorter events, 0.5 us)
Async XLA Ops:
  18.3 22.7 %all-to-all-start = ((bf16[16,2,1,4,2]{3,1,4,2,0:T(2,128)(2,1)}), bf16[16,2,1,4,2]{3,1,4,2,0:T(2,128)(2,1)S(1)}, u32[]{:S(2)}, u32[]{:S(2)}) async-start(bf16[16,2,1,4,2]{3,1,4,2,0:T(2,128)(2,1)} %copy.34), calls=%async_computation | async-start | bytes 32768 | tf_op jit(solution)/shard_map/all_to_all | solution.py:77
  41.1 26.8 %all-to-all-start.1 = ((bf16[16,1,2,1,4,3584]{5,4,2,3,1,0:T(4,128)(2,1)}), bf16[16,1,2,1,4,3584]{5,4,2,3,1,0:T(4,128)(2,1)S(1)}, u32[]{:S(2)}, u32[]{:S(2)}) async-start(bf16[16,1,2,1,4,3584]{5,4,2,3,1,0:T(4,128)(2,1)} %constant_dynamic-update-slice_fusion), calls=%async_computation.1 | async-start | bytes 1835008 | tf_op jit(solution)/shard_map/all_to_all | solution.py:67
  96.0 26.7 %all-to-all-start.3 = ((f32[16,4,3584]{2,1,0:T(4,128)}), f32[16,4,3584]{2,1,0:T(4,128)S(1)}, u32[]{:S(2)}, u32[]{:S(2)}) async-start(f32[16,4,3584]{2,1,0:T(4,128)} %reshape.103), calls=%async_computation.3 | async-start | bytes 1835008 | tf_op jit(solution)/shard_map/all_to_all | solution.py:92
  101.9 35.9 %reduce-scatter.2.cloned.1.call-start = ((), (), s32[]{:S(2)}) async-start(), calls=%async_computation.5 | async-start | bytes 344064 | tf_op jit(solution)/shard_map/reduce_scatter | solution.py:98
Sparse Core Ops, SparseCore 0:
  125.9 11.8 reduce-scatter.1
